TPU v7x, 32 devices: a whole 2x2x4 slice. The times are simulated.
32 devices in a mesh: gx: 2 (over y), gy: 4 (over x, core), gz: 4 (over z).
Axes of the slice: x: 2, y: 2, z: 4, core: 2. Of those that a mesh axis runs over, the one named last changes fastest.
Arguments:
- snapshots: bfloat16 [16, 64, 64, 256], P('gx', 'gy', 'gz'), may hold values from -1500 to 1500
- sketch: float32 [256, 256], replicated, may hold values from -0.5 to 1.5
- velocity: float32 [3, 16, 64, 64], P(None, 'gx', 'gy', 'gz'), may hold values from -4 to 4
- viscosity: float32 [16, 64, 64], P('gx', 'gy', 'gz'), may hold values from 0.2 to 2
Outputs:
- applied_modes: bfloat16 [16, 64, 64, 256], P('gx', 'gy', 'gz')
- reduced: float32 [256, 256], replicated
All inputs are finite; a program needn't handle non-finite values.
Results may differ from a plain program's by a relative error of at most 0.0015.
The roundings to bfloat16 on the way count: a program that leaves them out, or rounds other values in their place, can miss the bound.
Values may be sent and summed in bfloat16 or wider, within the bound.
No kernel may reach another device: no remote copies, remote signals or barrier semaphores. Data moves between devices by JAX's collectives and lax.ppermute only.
A program may use at most 64 MiB of HBM per device.

v0:
```python
import jax
import jax.numpy as jnp
from jax import lax
from jax.sharding import PartitionSpec as P


def padded_2(cells, sides, width):
    for axis, dim in sides:
        count = lax.axis_size(axis)
        ends = count - 1
        head = lax.slice_in_dim(cells, 0, width, axis=dim)
        tail = lax.slice_in_dim(cells, cells.shape[dim] - width, cells.shape[dim], axis=dim)
        cells = jnp.concatenate(
            [
                lax.ppermute(tail, axis, [(i, (i + 1) % count) for i in range(ends)]),
                cells,
                lax.ppermute(head, axis, [((i + 1) % count, i) for i in range(ends)]),
            ],
            axis=dim,
        )
    return cells


def apply_operator(padded, velocity, viscosity):
    centre = padded[1:-1, 1:-1, 1:-1]
    east_side = padded[2:, 1:-1, 1:-1]
    west_side = padded[:-2, 1:-1, 1:-1]
    north_side = padded[1:-1, 2:, 1:-1]
    south_side = padded[1:-1, :-2, 1:-1]
    upper_side = padded[1:-1, 1:-1, 2:]
    lower_side = padded[1:-1, 1:-1, :-2]
    neighbours = east_side + west_side + north_side + south_side + upper_side + lower_side
    viscous_term = viscosity[..., None] * (6.0 * centre - neighbours)
    flow_term = velocity[0][..., None] * (east_side - west_side)
    flow_term = flow_term + velocity[1][..., None] * (north_side - south_side)
    flow_term = flow_term + velocity[2][..., None] * (upper_side - lower_side)
    return viscous_term + 0.5 * flow_term


def inner_rows(left_rows, right_rows, precision):
    return lax.dot_general(
        left_rows,
        right_rows,
        (((0,), (0,)), ((), ())),
        precision=precision,
        preferred_element_type=jnp.float32,
    )


def per_device(snapshots, sketch, velocity, viscosity):
    highest = lax.Precision.HIGHEST
    columns = sketch.shape[0]
    cells_x, cells_y, cells_z = (snapshots.shape[0], snapshots.shape[1], snapshots.shape[2])
    ncells = (
        cells_x
        * cells_y
        * cells_z
        * lax.axis_size("gx")
        * lax.axis_size("gy")
        * lax.axis_size("gz")
    )
    sketched = jnp.dot(
        snapshots.reshape(-1, columns).astype(jnp.float32), sketch, precision=highest
    ).astype(jnp.bfloat16)
    local_gram = inner_rows(sketched, sketched, None) / ncells
    gram_matrix = lax.psum(local_gram, ("gx", "gy", "gz"))
    lower_factor = jnp.linalg.cholesky(gram_matrix)
    inverse = jax.scipy.linalg.solve_triangular(
        lower_factor, jnp.eye(columns, dtype=jnp.float32), lower=True
    )
    mode_rows = jnp.dot(sketched.astype(jnp.float32), inverse.T, precision=highest)
    mode_field = mode_rows.reshape(cells_x, cells_y, cells_z, columns)
    padded_modes = padded_2(mode_field, (("gx", 0), ("gy", 1), ("gz", 2)), 1)
    image_rows = apply_operator(padded_modes, velocity, viscosity).reshape(-1, columns)
    local_reduced = inner_rows(mode_rows, image_rows, highest) / ncells
    reduced = lax.psum(local_reduced, ("gx", "gy", "gz"))
    applied_modes = image_rows.reshape(cells_x, cells_y, cells_z, columns).astype(jnp.bfloat16)
    return (applied_modes, reduced)


def solution(mesh):
    in_specs = (P("gx", "gy", "gz", None), P(), P(None, "gx", "gy", "gz"), P("gx", "gy", "gz"))
    out_specs = (P("gx", "gy", "gz", None), P())
    return jax.shard_map(
        per_device, mesh=mesh, in_specs=in_specs, out_specs=out_specs, check_vma=False
    )
```

profile of v0, /device:TPU:0, one launch (start us, length us, event | category | flops | bytes accessed | tf_op | source)
XLA Modules:
  0.0 380.9 jit_solution(7893172982498539869)
XLA Ops:
  7.2 1.2 copy-done
  8.4 2.0 convolution_convert_fusion
  10.4 1.2 convolution_multiply_fusion.1
  11.7 131.6 %all-reduce.4.cloned.1.call-done = f32[256,256]{0,1:T(8,128)} async-done(((f32[256,256]{0,1:T(8,128)}), f32[256,256]{0,1:T(8,128)}) %all-reduce.4.cloned.1.call-update) | async-done | bytes 262160 | tf_op jit(solution)/shard_map/psum | solution.py:66
  143.3 1.1 copy.7
  144.4 1.0 fusion.4
  145.4 11.7 %cholesky.50 = f32[128,128]{1,0:T(8,128)S(1)} custom-call(f32[128,128]{1,0:T(8,128)S(1)} %cholesky.118), custom_call_target="Cholesky" | custom-call | tf_op jit(solution)/shard_map/jit(cholesky)/cholesky | solution.py:67
  157.2 9.8 %custom-call.15 = f32[1,128,128]{1,2,0:T(8,128)S(1)} custom-call(f32[1,128,128]{2,1,0:T(8,128)S(1)} %get-tuple-element.36), custom_call_target="InvertDiagBlocksLowerTriangular" | custom-call | tf_op jit(solution)/shard_map/jit(cholesky)/cholesky | solution.py:67
  167.5 11.7 %cholesky.105 = f32[128,128]{1,0:T(8,128)S(1)} custom-call(f32[128,128]{1,0:T(8,128)S(1)} %convolution_subtract_fusion.1), custom_call_target="Cholesky" | custom-call | tf_op jit(solution)/shard_map/jit(cholesky)/cholesky | solution.py:67
  179.2 0.7 compare_reduce_fusion
  181.4 4.2 %while.1 = (s32[]{:T(128)}, f32[256,256]{1,0:T(8,128)S(1)}, s32[2,2]{1,0:T(2,128)S(1)}, f32[2,128,128]{2,1,0:T(8,128)S(1)}, s32[]{:T(128)}) while((s32[]{:T(128)}, f32[256,256]{1,0:T(8,128)S(1)}, s32[2,2]{1,0:T(2,128)S(1)}, f32[2,128,128]{2,1,0:T(8,128)S(1)}, s32[]{:T(128)}) %tuple.34), condition=%wide.while_cond, body=%wide.while_body.sunk | while | flops 2 | bytes 131189 | solution.py:68
  181.5 0.6 fusion.28
  182.1 1.4 bitcast_dynamic-update-slice_fusion.2
  183.6 0.6 fusion.28
  184.2 1.4 bitcast_dynamic-update-slice_fusion.2
  185.6 19.7 %custom-call.16 = f32[2,128,128]{1,2,0:T(8,128)S(1)} custom-call(f32[2,128,128]{2,1,0:T(8,128)S(1)} %get-tuple-element.9), custom_call_target="InvertDiagBlocksLowerTriangular" | custom-call | tf_op jit(solution)/shard_map/jit(_solve_triangular)/triangular_solve | solution.py:68
  206.1 1.1 fusion
  207.2 1.3 collective-permute-start
  208.5 4.6 %collective-permute-start.1 = (f32[1,16,16,256]{3,2,1,0:T(8,128)S(1)}, f32[1,16,16,256]{3,2,1,0:T(8,128)S(1)}, u32[]{:S(2)}, u32[]{:S(2)}) collective-permute-start(f32[1,16,16,256]{3,2,1,0:T(8,128)S(1)} %bitcast.54), channel_id=1, source_target_pairs={{0,16},{1,17},{2,18},{3,19},{4,20},{5,21},{6,22},{7,23},{8,24},{9,... | collective-permute-start | bytes 786440 | tf_op jit(solution)/shard_map/ppermute | solution.py:15
  213.1 3.3 collective-permute-done
  216.4 1.2 collective-permute-done.1
  217.6 1.4 collective-permute-start.3
  219.1 1.3 collective-permute-start.2
  220.4 3.7 collective-permute-done.2
  224.3 1.3 collective-permute-start.4
  225.6 4.6 %collective-permute-start.5 = (f32[10,18,1,256]{3,2,1,0:T(1,128)S(1)}, f32[10,18,1,256]{3,2,1,0:T(1,128)S(1)}, u32[]{:S(2)}, u32[]{:S(2)}) collective-permute-start(f32[10,18,1,256]{3,2,1,0:T(1,128)S(1)} %get-tuple-element.25), channel_id=1, source_target_pairs={{0,1},{1,2},{2,3},{4,5},{5,6},{6,7},{8,9},{9,10},{10,11},{12,13},{... | collective-permute-start | bytes 552968 | tf_op jit(solution)/shard_map/ppermute | solution.py:15
  230.2 1.5 collective-permute-done.4
  231.7 1.5 collective-permute-done.5
  233.2 4.6 %fusion.13 = (bf16[8,16,16,256]{3,2,1,0:T(8,128)(2,1)}, f32[8,16,16,256]{3,2,1,0:T(8,128)S(1)}) fusion(f32[8,16,16]{2,1,0:T(8,128)S(1)} %get-tuple-element.31, f32[8,16,16]{2,1,0:T(8,128)S(1)} %get-tuple-element.32, f32[8,16,16]{2,1,0:T(8,128)S(1)} %get-tuple-element.30, f32[10,1,16,256]{3,2,1,0:T(8,128)S(1)} %collective-permute-done.2, ...), kind=kLoop, calls=%fused_computation.66 | loop fusion | flops 19398656 | bytes 6496256 | tf_op jit(solution)/shard_map/convert_element_type | solution.py:77
  237.8 4.3 %convolution_multiply_fusion = f32[256,256]{0,1:T(8,128)} fusion(f32[2048,256]{1,0:T(8,128)S(1)} %fusion, f32[2048,256]{1,0:T(8,128)S(1)} %bitcast.53), kind=kOutput, calls=%fused_computation.22 | convolution fusion | flops 1610678272 | bytes 4456448 | tf_op jit(solution)/shard_map/dot_general | solution.py:41
  242.1 130.2 %all-reduce.6.cloned.1.call-done = f32[256,256]{0,1:T(8,128)} async-done(((f32[256,256]{0,1:T(8,128)}), f32[256,256]{0,1:T(8,128)}) %all-reduce.6.cloned.1.call-update) | async-done | bytes 262160 | tf_op jit(solution)/shard_map/psum | solution.py:76
  372.3 1.8 copy.9
  (30 shorter events, 2.0 us)
Async XLA Ops:
  7.2 1.2 copy-start
  7.2 136.1 %all-reduce.4.cloned.1.call-start = ((), (), s32[]{:S(2)}) async-start(), calls=%async_computation | async-start | bytes 524288 | tf_op jit(solution)/shard_map/psum | solution.py:66
  11.6 360.7 %all-reduce.6.cloned.1.call-start = ((), (), s32[]{:S(2)}) async-start(), calls=%async_computation.1 | async-start | bytes 524288 | tf_op jit(solution)/shard_map/psum | solution.py:76
  207.2 9.1 %collective-permute-start = (f32[1,16,16,256]{3,2,1,0:T(8,128)S(1)}, f32[1,16,16,256]{3,2,1,0:T(8,128)S(1)}, u32[]{:S(2)}, u32[]{:S(2)}) collective-permute-start(f32[1,16,16,256]{3,2,1,0:T(8,128)S(1)} %bitcast.55), channel_id=1, source_target_pairs={{16,0},{17,1},{18,2},{19,3},{20,4},{21,5},{22,6},{23,7},{24,8},{25... | collective-permute-start | bytes 786440 | tf_op jit(solution)/shard_map/ppermute | solution.py:17
  208.5 9.0 %collective-permute-start.1 = (f32[1,16,16,256]{3,2,1,0:T(8,128)S(1)}, f32[1,16,16,256]{3,2,1,0:T(8,128)S(1)}, u32[]{:S(2)}, u32[]{:S(2)}) collective-permute-start(f32[1,16,16,256]{3,2,1,0:T(8,128)S(1)} %bitcast.54), channel_id=1, source_target_pairs={{0,16},{1,17},{2,18},{3,19},{4,20},{5,21},{6,22},{7,23},{8,24},{9,... | collective-permute-start | bytes 786440 | tf_op jit(solution)/shard_map/ppermute | solution.py:15
  217.6 12.6 %copy-start.1 = (f32[3,8,16,16]{3,2,1,0:T(8,128)S(1)}, f32[3,8,16,16]{3,2,1,0:T(8,128)}, u32[]{:S(2)}) copy-start(f32[3,8,16,16]{3,2,1,0:T(8,128)} %param.6) | copy-start | bytes 73732
  217.6 15.6 %copy-start.2 = (f32[8,16,16]{2,1,0:T(8,128)S(1)}, f32[8,16,16]{2,1,0:T(8,128)}, u32[]{:S(2)}) copy-start(f32[8,16,16]{2,1,0:T(8,128)} %param.7) | copy-start | bytes 24580
  217.6 2.7 collective-permute-start.3
  219.1 5.0 %collective-permute-start.2 = (f32[10,1,16,256]{3,2,1,0:T(8,128)S(1)}, f32[10,1,16,256]{3,2,1,0:T(8,128)S(1)}, u32[]{:S(2)}, u32[]{:S(2)}) collective-permute-start(f32[10,1,16,256]{3,2,1,0:T(8,128)S(1)} %get-tuple-element.27), channel_id=1, source_target_pairs={{4,0},{8,4},{12,8},{5,1},{9,5},{13,9},{6,2},{10,6},{14,10},{7,3},{... | collective-permute-start | bytes 491528 | tf_op jit(solution)/shard_map/ppermute | solution.py:17
  224.3 7.4 %collective-permute-start.4 = (f32[10,18,1,256]{3,2,1,0:T(1,128)S(1)}, f32[10,18,1,256]{3,2,1,0:T(1,128)S(1)}, u32[]{:S(2)}, u32[]{:S(2)}) collective-permute-start(f32[10,18,1,256]{3,2,1,0:T(1,128)S(1)} %get-tuple-element.24), channel_id=1, source_target_pairs={{1,0},{2,1},{3,2},{5,4},{6,5},{7,6},{9,8},{10,9},{11,10},{13,12},{... | collective-permute-start | bytes 552968 | tf_op jit(solution)/shard_map/ppermute | solution.py:17
  225.6 7.6 %collective-permute-start.5 = (f32[10,18,1,256]{3,2,1,0:T(1,128)S(1)}, f32[10,18,1,256]{3,2,1,0:T(1,128)S(1)}, u32[]{:S(2)}, u32[]{:S(2)}) collective-permute-start(f32[10,18,1,256]{3,2,1,0:T(1,128)S(1)} %get-tuple-element.25), channel_id=1, source_target_pairs={{0,1},{1,2},{2,3},{4,5},{5,6},{6,7},{8,9},{9,10},{10,11},{12,13},{... | collective-permute-start | bytes 552968 | tf_op jit(solution)/shard_map/ppermute | solution.py:15
Sparse Core Ops, SparseCore 0:
  14.1 129.2 all-reduce.3
  242.2 130.0 all-reduce.5
where the time goes:
time: 381 us
  waiting for transfers between devices  273 us (72%)
  other arithmetic  59.6 us (16%)
  between operations  15.6 us (4%)
  starting transfers between devices  14.5 us (4%)
  matrix products  9.81 us (3%)
  local copies, waits for them, and re-layouts  8.22 us (2%)
    psum x1, waiting for transfers between devices, per_device(): gram_matrix = lax.psum(local_gram, ('gx', 'gy', 'gz'))  132 us
    psum x1, waiting for transfers between devices, per_device(): reduced = lax.psum(local_reduced, ('gx', 'gy', 'gz'))  130 us
    another operation x6, other arithmetic, per_device(): lower_factor = jnp.linalg.cholesky(gram_matrix)  34 us
    another operation x3, other arithmetic, per_device(): jax.scipy.linalg.solve_triangular(lower_factor, jnp.eye(columns, dtype=jn...  19.7 us
    ppermute x3, starting transfers between devices, padded_2(): lax.ppermute(tail, axis, [(i, (i + 1) % count) for i in range(ends)])  10.6 us
    ppermute x3, waiting for transfers between devices, padded_2(): lax.ppermute(head, axis, [((i + 1) % count, i) for i in range(ends)])  8.48 us
  transfers between devices with their start and end apart: 8, of which 7 were waited for; matrix products, arithmetic and copies ran while one was open for 0% of the time, Pallas kernels for 0%

commit v1 on v0

--- a/solution.py
+++ b/solution.py
@@ -73,7 +73,7 @@
     padded_modes = padded_2(mode_field, (("gx", 0), ("gy", 1), ("gz", 2)), 1)
     image_rows = apply_operator(padded_modes, velocity, viscosity).reshape(-1, columns)
     local_reduced = inner_rows(mode_rows, image_rows, highest) / ncells
-    reduced = lax.psum(local_reduced, ("gx", "gy", "gz"))
+    reduced = jnp.sum(lax.all_gather(local_reduced, ("gx", "gy", "gz")), axis=0)
     applied_modes = image_rows.reshape(cells_x, cells_y, cells_z, columns).astype(jnp.bfloat16)
     return (applied_modes, reduced)
 

time: 381 us -> 347 us (0.911)
  waiting for transfers between devices: 273 us -> 230 us
  local copies, waits for them, and re-layouts: 8.22 us -> 14.1 us
    psum x1 -> x0, waiting for transfers between devices: 130 us -> none  [per_device(): reduced = lax.psum(local_reduced, ('gx', 'gy', 'gz'))]
    all_gather x0 -> x1, waiting for transfers between devices: none -> 87.7 us  [per_device(): reduced = jnp.sum(lax.all_gather(local_reduced, ('gx', 'gy', 'gz')), axis=0)]
    unnamed x7 -> x8, local copies, waits for them, and re-layouts: 2.97 us -> 8.86 us
where the time goes in v1:
time: 347 us; the launch traced here: 346 us
  waiting for transfers between devices  230 us (66%)
  other arithmetic  61.5 us (18%)
  between operations  15.6 us (4%)
  starting transfers between devices  14.5 us (4%)
  local copies, waits for them, and re-layouts  14.1 us (4%)
  matrix products  9.81 us (3%)
    psum x1, waiting for transfers between devices, per_device(): gram_matrix = lax.psum(local_gram, ('gx', 'gy', 'gz'))  132 us
    all_gather x1, waiting for transfers between devices, per_device(): reduced = jnp.sum(lax.all_gather(local_reduced, ('gx', 'gy', 'gz')), axis=0)  87.7 us
    another operation x6, other arithmetic, per_device(): lower_factor = jnp.linalg.cholesky(gram_matrix)  34 us
    another operation x3, other arithmetic, per_device(): jax.scipy.linalg.solve_triangular(lower_factor, jnp.eye(columns, dtype=jn...  19.7 us
    ppermute x3, starting transfers between devices, padded_2(): lax.ppermute(tail, axis, [(i, (i + 1) % count) for i in range(ends)])  10.6 us
    unnamed x8, local copies, waits for them, and re-layouts  8.86 us
    ppermute x3, waiting for transfers between devices, padded_2(): lax.ppermute(head, axis, [((i + 1) % count, i) for i in range(ends)])  8.48 us
  transfers between devices with their start and end apart: 8, of which 7 were waited for; matrix products, arithmetic and copies ran while one was open for 0% of the time, Pallas kernels for 0%

profile of v1, /device:TPU:0, one launch (start us, length us, event | category | flops | bytes accessed | tf_op | source)
XLA Modules:
  0.0 346.2 jit_solution(11412699703965742877)
XLA Ops:
  7.2 1.2 copy-done
  8.4 2.0 convolution_convert_fusion
  10.4 1.2 convolution_multiply_fusion.1
  11.7 131.6 %all-reduce.3.cloned.1.call-done = f32[256,256]{0,1:T(8,128)} async-done(((f32[256,256]{0,1:T(8,128)}), f32[256,256]{0,1:T(8,128)}) %all-reduce.3.cloned.1.call-update) | async-done | bytes 262160 | tf_op jit(solution)/shard_map/psum | solution.py:66
  143.3 1.1 copy.10
  144.4 1.0 fusion.4
  145.4 11.7 %cholesky.50 = f32[128,128]{1,0:T(8,128)S(1)} custom-call(f32[128,128]{1,0:T(8,128)S(1)} %cholesky.118), custom_call_target="Cholesky" | custom-call | tf_op jit(solution)/shard_map/jit(cholesky)/cholesky | solution.py:67
  157.2 9.8 %custom-call.15 = f32[1,128,128]{1,2,0:T(8,128)S(1)} custom-call(f32[1,128,128]{2,1,0:T(8,128)S(1)} %get-tuple-element.36), custom_call_target="InvertDiagBlocksLowerTriangular" | custom-call | tf_op jit(solution)/shard_map/jit(cholesky)/cholesky | solution.py:67
  167.5 11.7 %cholesky.105 = f32[128,128]{1,0:T(8,128)S(1)} custom-call(f32[128,128]{1,0:T(8,128)S(1)} %convolution_subtract_fusion.1), custom_call_target="Cholesky" | custom-call | tf_op jit(solution)/shard_map/jit(cholesky)/cholesky | solution.py:67
  179.2 0.7 compare_reduce_fusion
  181.4 4.2 %while.1 = (s32[]{:T(128)}, f32[256,256]{1,0:T(8,128)S(1)}, s32[2,2]{1,0:T(2,128)S(1)}, f32[2,128,128]{2,1,0:T(8,128)S(1)}, s32[]{:T(128)}) while((s32[]{:T(128)}, f32[256,256]{1,0:T(8,128)S(1)}, s32[2,2]{1,0:T(2,128)S(1)}, f32[2,128,128]{2,1,0:T(8,128)S(1)}, s32[]{:T(128)}) %tuple.34), condition=%wide.while_cond, body=%wide.while_body.sunk | while | flops 2 | bytes 131189 | solution.py:68
  182.1 1.4 bitcast_dynamic-update-slice_fusion.2
  184.2 1.4 bitcast_dynamic-update-slice_fusion.2
  185.6 19.7 %custom-call.16 = f32[2,128,128]{1,2,0:T(8,128)S(1)} custom-call(f32[2,128,128]{2,1,0:T(8,128)S(1)} %get-tuple-element.9), custom_call_target="InvertDiagBlocksLowerTriangular" | custom-call | tf_op jit(solution)/shard_map/jit(_solve_triangular)/triangular_solve | solution.py:68
  206.1 1.1 fusion
  207.2 1.3 collective-permute-start
  208.5 4.6 %collective-permute-start.1 = (f32[1,16,16,256]{3,2,1,0:T(8,128)S(1)}, f32[1,16,16,256]{3,2,1,0:T(8,128)S(1)}, u32[]{:S(2)}, u32[]{:S(2)}) collective-permute-start(f32[1,16,16,256]{3,2,1,0:T(8,128)S(1)} %bitcast.60), channel_id=1, source_target_pairs={{0,16},{1,17},{2,18},{3,19},{4,20},{5,21},{6,22},{7,23},{8,24},{9,... | collective-permute-start | bytes 786440 | tf_op jit(solution)/shard_map/ppermute | solution.py:15
  213.1 3.3 collective-permute-done
  216.4 1.2 collective-permute-done.1
  217.6 1.4 collective-permute-start.3
  219.1 1.3 collective-permute-start.2
  220.4 3.7 %collective-permute-done.2 = f32[10,1,16,256]{3,2,1,0:T(8,128)S(1)} collective-permute-done((f32[10,1,16,256]{3,2,1,0:T(8,128)S(1)}, f32[10,1,16,256]{3,2,1,0:T(8,128)S(1)}, u32[]{:S(2)}, u32[]{:S(2)}) %collective-permute-start.2) | collective-permute-done | bytes 163872 | tf_op jit(solution)/shard_map/ppermute | solution.py:17
  224.3 1.3 collective-permute-start.4
  225.6 4.6 %collective-permute-start.5 = (f32[10,18,1,256]{3,2,1,0:T(1,128)S(1)}, f32[10,18,1,256]{3,2,1,0:T(1,128)S(1)}, u32[]{:S(2)}, u32[]{:S(2)}) collective-permute-start(f32[10,18,1,256]{3,2,1,0:T(1,128)S(1)} %get-tuple-element.25), channel_id=1, source_target_pairs={{0,1},{1,2},{2,3},{4,5},{5,6},{6,7},{8,9},{9,10},{10,11},{12,13},{... | collective-permute-start | bytes 552968 | tf_op jit(solution)/shard_map/ppermute | solution.py:15
  230.2 1.5 collective-permute-done.4
  231.7 1.5 collective-permute-done.5
  233.2 4.6 %fusion.13 = (bf16[8,16,16,256]{3,2,1,0:T(8,128)(2,1)}, f32[8,16,16,256]{3,2,1,0:T(8,128)S(1)}) fusion(f32[8,16,16]{2,1,0:T(8,128)S(1)} %get-tuple-element.31, f32[8,16,16]{2,1,0:T(8,128)S(1)} %get-tuple-element.32, f32[8,16,16]{2,1,0:T(8,128)S(1)} %get-tuple-element.30, f32[10,1,16,256]{3,2,1,0:T(8,128)S(1)} %collective-permute-done.2, ...), kind=kLoop, calls=%fused_computation.67 | loop fusion | flops 19398656 | bytes 6496256 | tf_op jit(solution)/shard_map/convert_element_type | solution.py:77
  237.8 4.3 %convolution_multiply_fusion = f32[256,256]{0,1:T(8,128)} fusion(f32[2048,256]{1,0:T(8,128)S(1)} %fusion, f32[2048,256]{1,0:T(8,128)S(1)} %bitcast.59), kind=kOutput, calls=%fused_computation.23 | convolution fusion | flops 1610678272 | bytes 4456448 | tf_op jit(solution)/shard_map/dot_general | solution.py:41
  242.1 87.7 %all-gather.3.cloned.1.call-done = f32[8192,256]{0,1:T(8,128)} async-done(((f32[256,256]{0,1:T(8,128)}), f32[8192,256]{0,1:T(8,128)}) %all-gather.3.cloned.1.call-update) | async-done | bytes 8388624 | tf_op jit(solution)/shard_map/all_gather | solution.py:76
  329.8 6.8 %copy.15 = f32[32,8,32,256]{3,2,1,0:T(8,128)S(1)} copy(f32[32,8,32,256]{3,1,2,0:T(8,128)} %bitcast.58) | data formatting | bytes 16777216
  336.6 1.9 bitcast_reduce_fusion
  338.5 0.8 copy.12
  (32 shorter events, 3.2 us)
Async XLA Ops:
  7.2 1.2 copy-start
  7.2 136.1 %all-reduce.3.cloned.1.call-start = ((), (), s32[]{:S(2)}) async-start(), calls=%async_computation | async-start | bytes 524288 | tf_op jit(solution)/shard_map/psum | solution.py:66
  11.6 318.2 %all-gather.3.cloned.1.call-start = ((), (), s32[]{:S(2)}) async-start(), calls=%async_computation.1 | async-start | bytes 8650752 | tf_op jit(solution)/shard_map/all_gather | solution.py:76
  207.2 9.1 %collective-permute-start = (f32[1,16,16,256]{3,2,1,0:T(8,128)S(1)}, f32[1,16,16,256]{3,2,1,0:T(8,128)S(1)}, u32[]{:S(2)}, u32[]{:S(2)}) collective-permute-start(f32[1,16,16,256]{3,2,1,0:T(8,128)S(1)} %bitcast.61), channel_id=1, source_target_pairs={{16,0},{17,1},{18,2},{19,3},{20,4},{21,5},{22,6},{23,7},{24,8},{25... | collective-permute-start | bytes 786440 | tf_op jit(solution)/shard_map/ppermute | solution.py:17
  208.5 9.0 %collective-permute-start.1 = (f32[1,16,16,256]{3,2,1,0:T(8,128)S(1)}, f32[1,16,16,256]{3,2,1,0:T(8,128)S(1)}, u32[]{:S(2)}, u32[]{:S(2)}) collective-permute-start(f32[1,16,16,256]{3,2,1,0:T(8,128)S(1)} %bitcast.60), channel_id=1, source_target_pairs={{0,16},{1,17},{2,18},{3,19},{4,20},{5,21},{6,22},{7,23},{8,24},{9,... | collective-permute-start | bytes 786440 | tf_op jit(solution)/shard_map/ppermute | solution.py:15
  217.6 12.6 %copy-start.1 = (f32[3,8,16,16]{3,2,1,0:T(8,128)S(1)}, f32[3,8,16,16]{3,2,1,0:T(8,128)}, u32[]{:S(2)}) copy-start(f32[3,8,16,16]{3,2,1,0:T(8,128)} %param.6) | copy-start | bytes 73732
  217.6 15.6 %copy-start.2 = (f32[8,16,16]{2,1,0:T(8,128)S(1)}, f32[8,16,16]{2,1,0:T(8,128)}, u32[]{:S(2)}) copy-start(f32[8,16,16]{2,1,0:T(8,128)} %param.7) | copy-start | bytes 24580
  217.6 2.7 collective-permute-start.3
  219.1 5.0 %collective-permute-start.2 = (f32[10,1,16,256]{3,2,1,0:T(8,128)S(1)}, f32[10,1,16,256]{3,2,1,0:T(8,128)S(1)}, u32[]{:S(2)}, u32[]{:S(2)}) collective-permute-start(f32[10,1,16,256]{3,2,1,0:T(8,128)S(1)} %get-tuple-element.27), channel_id=1, source_target_pairs={{4,0},{8,4},{12,8},{5,1},{9,5},{13,9},{6,2},{10,6},{14,10},{7,3},{... | collective-permute-start | bytes 491528 | tf_op jit(solution)/shard_map/ppermute | solution.py:17
  224.3 7.4 %collective-permute-start.4 = (f32[10,18,1,256]{3,2,1,0:T(1,128)S(1)}, f32[10,18,1,256]{3,2,1,0:T(1,128)S(1)}, u32[]{:S(2)}, u32[]{:S(2)}) collective-permute-start(f32[10,18,1,256]{3,2,1,0:T(1,128)S(1)} %get-tuple-element.24), channel_id=1, source_target_pairs={{1,0},{2,1},{3,2},{5,4},{6,5},{7,6},{9,8},{10,9},{11,10},{13,12},{... | collective-permute-start | bytes 552968 | tf_op jit(solution)/shard_map/ppermute | solution.py:17
  225.6 7.6 %collective-permute-start.5 = (f32[10,18,1,256]{3,2,1,0:T(1,128)S(1)}, f32[10,18,1,256]{3,2,1,0:T(1,128)S(1)}, u32[]{:S(2)}, u32[]{:S(2)}) collective-permute-start(f32[10,18,1,256]{3,2,1,0:T(1,128)S(1)} %get-tuple-element.25), channel_id=1, source_target_pairs={{0,1},{1,2},{2,3},{4,5},{5,6},{6,7},{8,9},{9,10},{10,11},{12,13},{... | collective-permute-start | bytes 552968 | tf_op jit(solution)/shard_map/ppermute | solution.py:15
Sparse Core Ops, SparseCore 0:
  14.1 129.2 all-reduce.2
  242.2 87.5 all-gather.2
